TPU v7x, 512 devices: a whole 4x8x8 slice. The times are simulated.
512 devices in a mesh: aux: 8 (over z), ao: 16 (over y, core), orb: 4 (over x).
Axes of the slice: x: 4, y: 8, z: 8, core: 2. Of those that a mesh axis runs over, the one named last changes fastest.
Arguments:
- integrals: bfloat16 [128, 16, 4, 128, 128], P('aux', 'ao', None, 'orb'), may hold values from -6 to 6
- partner: int32 [16, 4], P('ao'), may hold values from 0 to 15
- pair_count: int32 [16], P('ao'), may hold values from 1 to 4
- occupied_coeff: bfloat16 [2048, 512], P('ao', 'orb'), may hold values from -0.25 to 0.25
- occupied_domain: int32 [16, 4], P('ao', 'orb'), may hold values 0 or 1
- virtual_coeff: bfloat16 [2048, 8192], P('aux', 'ao'), may hold values from -0.125 to 0.125
- virtual_domain: int32 [16, 64], P(None, 'ao'), may hold values 0 or 1
Outputs:
- transformed: bfloat16 [128, 512, 8192], P('aux', 'orb', 'ao')
All inputs are finite; a program needn't handle non-finite values. No bound on the sum of `occupied_domain` or of `virtual_domain` on one device may be relied on, other than what follows from the above.
Results may differ from a plain program's by a relative error of at most 0.0049.
Values may be sent and summed in bfloat16 or wider, within the bound.
A program may use at most 64 MiB of HBM per device.

v0:
```python
import jax
import jax.numpy as jnp
from jax import lax
from jax.sharding import PartitionSpec as P


def local(
    integrals, partner, pair_count, occupied_coeff, occupied_domain, virtual_coeff, virtual_domain
):
    block_size = integrals.shape[4]
    slab_rows = integrals.shape[0]
    local_blocks = integrals.shape[1]
    slot_count = integrals.shape[2]
    occ_width = occupied_coeff.shape[1]
    domain_wire = occupied_domain.astype(jnp.bfloat16)
    all_occ, all_domain = (
        lax.all_gather(occupied_coeff, "ao", axis=0, tiled=True),
        lax.all_gather(domain_wire, "ao", axis=0, tiled=True),
    )
    occ_mask = jnp.repeat(jnp.repeat(all_domain, block_size, axis=0), block_size, axis=1)
    occ_masked = all_occ * occ_mask
    block_total = all_domain.shape[0]
    picked = occ_masked.reshape(block_total, block_size, occ_width)[partner]
    slots = jnp.arange(slot_count, dtype=jnp.int32)
    live = (slots[None, :] < pair_count[:, None]).astype(jnp.bfloat16)
    picked = picked * live[:, :, None, None]
    all_columns = lax.all_to_all(picked, "orb", split_axis=2, concat_axis=3, tiled=True)
    partial_term = jnp.einsum(
        "nkri,pnkrv->pinv", all_columns, integrals, preferred_element_type=jnp.float32
    )
    half_wide = lax.psum_scatter(partial_term, "orb", scatter_dimension=1, tiled=True)
    half_local = half_wide.reshape(slab_rows, occ_width, local_blocks * block_size).astype(
        jnp.bfloat16
    )
    vir_rows = lax.all_gather(virtual_coeff, "aux", axis=0, tiled=True)
    vir_mask = jnp.repeat(
        jnp.repeat(virtual_domain, block_size, axis=0), block_size, axis=1
    ).astype(jnp.bfloat16)
    vir_masked = vir_rows * vir_mask
    vir_width = vir_masked.shape[1]
    piece = lax.all_gather(half_local, "ao", axis=2, tiled=True)
    count = piece.shape[2]
    flat = piece.reshape(slab_rows * occ_width, count)
    product = jnp.dot(flat, vir_masked, preferred_element_type=jnp.float32)
    result = product.reshape(slab_rows, occ_width, vir_width)
    return result.astype(jnp.bfloat16)


def solution(mesh):
    placed = (
        P("aux", "ao", None, "orb", None),
        P("ao", None),
        P("ao"),
        P("ao", "orb"),
        P("ao", "orb"),
        P("aux", "ao"),
        P(None, "ao"),
    )
    return jax.shard_map(
        local, mesh=mesh, in_specs=placed, out_specs=P("aux", "orb", "ao"), check_vma=False
    )
```

profile of v0, /device:TPU:1, one launch (start us, length us, event | category | flops | bytes accessed | tf_op | source)
XLA Modules:
  0.0 215.5 jit_solution(4892264346600140509)
XLA Ops:
  7.4 0.0 copy-start
  7.4 0.0 reduce-scatter.2.cloned.1.call-start
  8.7 0.7 fusion.11
  9.4 1.3 dynamic-slice
  10.7 0.7 dynamic-update-slice
  11.3 29.8 %all-reduce = bf16[16]{0:T(256)(128)(2,1)S(1)} all-reduce(bf16[16]{0:T(256)(128)(2,1)S(1)} %dynamic-update-slice), channel_id=1, replica_groups=mesh['aux'=8,'ao'=16,'orb'=4] {'ao'}, use_global_device_ids=true, to_apply=%add | all-reduce | flops 16 | bytes 64
  41.1 0.1 broadcast_bitcast_fusion
  41.2 16.4 %all_gather.14 = bf16[2048,128]{1,0:T(8,128)(2,1)S(1)} all-gather(bf16[128,128]{1,0:T(8,128)(2,1)} %param.10), channel_id=1, replica_groups=mesh['aux'=8,'ao'=16,'orb'=4] {'ao'}, dimensions={0}, use_global_device_ids=true | all-gather | bytes 557056 | tf_op jit(solution)/shard_map/all_gather | solution.py:17
  57.6 0.3 broadcast_multiply_fusion
  58.0 0.6 gather_fusion
  58.5 0.1 bitcast_multiply_fusion.1
  58.6 0.1 copy.14
  58.7 7.3 %all_to_all.15 = bf16[1,4,128,128]{3,1,0,2:T(4,128)(2,1)S(1)} all-to-all(bf16[1,4,128,128]{3,1,0,2:T(4,128)(2,1)S(1)} %copy.14), channel_id=1, replica_groups=mesh['aux'=8,'ao'=16,'orb'=4] {'orb'}, dimensions={2} | all-to-all | bytes 262144 | tf_op jit(solution)/shard_map/all_to_all | solution.py:27
  66.1 0.1 copy.16
  66.1 0.1 reshape.70
  66.2 0.0 copy-done
  66.2 2.7 %convolution_bitcast_fusion = f32[16,512,1,128]{3,1,0,2:T(8,128)} fusion(bf16[4,32,512,1]{2,1,0,3:T(8,128)(2,1)S(1)} %reshape.70, bf16[16,1,4,32,128]{4,3,2,1,0:T(8,128)(2,1)S(1)} %copy-done), kind=kOutput, calls=%fused_computation.3 | convolution fusion | flops 268435456 | bytes 4849664 | tf_op jit(solution)/shard_map/nkri,pnkrv->pinv/dot_general | solution.py:28
  68.9 0.0 reduce-scatter.2.cloned.1.call-update
  68.9 0.0 copy-start.1
  68.9 0.0 all-gather.4.cloned.1.call-start
  69.0 0.5 all-gather.4.cloned.1.call-update
  69.5 0.0 all-gather.6.cloned.1.call-start
  69.6 51.7 %reduce-scatter.2.cloned.1.call-done = f32[16,128,1,128]{3,1,0,2:T(8,128)} async-done(((f32[16,512,1,128]{3,1,0,2:T(8,128)}), f32[16,128,1,128]{3,1,0,2:T(8,128)}) %reduce-scatter.2.cloned.1.call-update) | async-done | bytes 1048592 | tf_op jit(solution)/shard_map/reduce_scatter | solution.py:31
  121.2 2.1 convert_element_type.34
  123.3 0.0 all-gather.6.cloned.1.call-update
  123.4 0.0 copy-done.1
  123.4 0.1 copy.17
  123.5 0.0 all-gather.4.cloned.1.call-done
  123.5 0.0 copy-start.2
  123.5 69.4 %all-gather.6.cloned.1.call-done = bf16[16,128,1,2048]{3,1,0,2:T(8,128)(2,1)} async-done(((bf16[16,128,1,128]{3,1,0,2:T(8,128)(2,1)}), bf16[16,128,1,2048]{3,1,0,2:T(8,128)(2,1)}) %all-gather.6.cloned.1.call-update) | async-done | bytes 8388624 | tf_op jit(solution)/shard_map/all_gather | solution.py:41
  192.9 0.1 broadcast_in_dim.21
  193.0 5.8 %broadcast_in_dim.22 = bf16[2048,4,128]{2,1,0:T(4,128)(2,1)S(1)} broadcast(bf16[2048,4]{1,0:T(8,128)(2,1)S(1)} %bitcast.47), dimensions={0,1} | broadcast | bytes 2113536 | tf_op jit(solution)/shard_map/broadcast_in_dim | solution.py:36
  198.7 0.0 copy-done.2
  198.8 9.3 %fusion.5 = bf16[16,128,512]{2,1,0:T(8,128)(2,1)} fusion(bf16[2048,512]{1,0:T(8,128)(2,1)S(1)} %copy-done.2, bf16[256,8,4,128]{3,2,1,0:T(4,128)(2,1)S(1)} %bitcast.46, bf16[16,128,1,2048]{3,1,0,2:T(8,128)(2,1)} %all-gather.6.cloned.1.call-done), kind=kOutput, calls=%fused_computation.7 | convolution fusion | flops 4297064448 | bytes 14680064 | tf_op jit(solution)/shard_map/dot_general | solution.py:44
  (5 shorter events, 0.0 us)
Async XLA Ops:
  7.4 58.8 %copy-start = (bf16[16,1,4,32,128]{4,3,2,1,0:T(8,128)(2,1)S(1)}, bf16[16,1,4,32,128]{4,3,2,1,0:T(8,128)(2,1)}, u32[]{:S(2)}) copy-start(bf16[16,1,4,32,128]{4,3,2,1,0:T(8,128)(2,1)} %param.7) | copy-start | bytes 1572868
  7.4 113.9 %reduce-scatter.2.cloned.1.call-start = ((), (), s32[]{:S(2)}) async-start(), calls=%async_computation.2 | async-start | bytes 5242880 | tf_op jit(solution)/shard_map/reduce_scatter | solution.py:31
  68.9 54.5 %copy-start.1 = (s32[16,4]{0,1:T(4,128)S(1)}, s32[16,4]{0,1:T(4,128)}, u32[]{:S(2)}) copy-start(s32[16,4]{0,1:T(4,128)} %param.13) | copy-start | bytes 772
  68.9 54.6 %all-gather.4.cloned.1.call-start = ((), (), s32[]{:S(2)}) async-start(), calls=%async_computation.3 | async-start | bytes 2359296 | tf_op jit(solution)/shard_map/all_gather | solution.py:35
  69.5 123.4 %all-gather.6.cloned.1.call-start = ((), (), s32[]{:S(2)}) async-start(), calls=%async_computation.4 | async-start | bytes 8912896 | tf_op jit(solution)/shard_map/all_gather | solution.py:41
  123.5 75.3 %copy-start.2 = (bf16[2048,512]{1,0:T(8,128)(2,1)S(1)}, bf16[2048,512]{1,0:T(8,128)(2,1)}, u32[]{:S(2)}) copy-start(bf16[2048,512]{1,0:T(8,128)(2,1)} %all-gather.4.cloned.1.call-done) | copy-start | bytes 6291460
Sparse Core Ops, SparseCore 0:
  69.0 52.1 reduce-scatter.1
Sparse Core Ops, SparseCore 1:
  71.5 40.2 all-gather.3
  123.5 69.4 all-gather.5
where the time goes:
time: 216 us
  waiting for transfers between devices  122 us (56%)
  blocking collectives  53.5 us (25%)
  between operations  16.3 us (8%)
  matrix products  12 us (6%)
  local copies, waits for them, and re-layouts  8.79 us (4%)
  other arithmetic  3.2 us (1%)
    all_gather x1, waiting for transfers between devices, local(): piece = lax.all_gather(half_local, 'ao', axis=2, tiled=True)  69.4 us
    reduce_scatter x1, waiting for transfers between devices, local(): lax.psum_scatter(partial_term, 'orb', scatter_dimension=1, tiled=True)  51.7 us
    unnamed x1, blocking collectives  29.8 us
    all_gather x1, blocking collectives, local(): lax.all_gather(occupied_coeff, 'ao', axis=0, tiled=True)  16.4 us
    dot_general x1, matrix products, local(): product = jnp.dot(flat, vir_masked, preferred_element_type=jnp.float32)  9.32 us
    all_to_all x1, blocking collectives, local(): lax.all_to_all(picked, 'orb', split_axis=2, concat_axis=3, tiled=True)  7.31 us
    broadcast_in_dim x1, local copies, waits for them, and re-layouts, local(): jnp.repeat(jnp.repeat(virtual_domain, block_size, axis=0), block_size, ax...  5.78 us
  transfers between devices with their start and end apart: 3, of which 2 were waited for; matrix products, arithmetic and copies ran while one was open for 1% of the time, Pallas kernels for 0%

commit v1 on v0

--- a/solution.py
+++ b/solution.py
@@ -38,7 +38,20 @@
     ).astype(jnp.bfloat16)
     vir_masked = vir_rows * vir_mask
     vir_width = vir_masked.shape[1]
-    piece = lax.all_gather(half_local, "ao", axis=2, tiled=True)
+
+    def stops_all_end(arr):
+        world_n = lax.axis_size("ao")
+        tray = [(u, (u + 1) % world_n) for u in range(world_n)]
+        table = [(u, (u - 1) % world_n) for u in range(world_n)]
+        shaped, v1 = ([arr], [arr])
+        for _ in range(world_n // 2):
+            shaped.append(lax.ppermute(shaped[-1], axis_name="ao", perm=tray))
+        for _ in tuple(range((world_n - 1) // 2)):
+            v1.append(lax.ppermute(v1[-1], axis_name="ao", perm=table))
+        ready = jnp.concatenate([*shaped[::-1], *v1[1:]], axis=2)
+        return jnp.roll(ready, (lax.axis_index("ao") - world_n // 2) * arr.shape[2], axis=2)
+
+    piece = stops_all_end(half_local)
     count = piece.shape[2]
     flat = piece.reshape(slab_rows * occ_width, count)
     product = jnp.dot(flat, vir_masked, preferred_element_type=jnp.float32)

time: 216 us -> 271 us (1.25)
  the two profiles are of different devices: /device:TPU:1 before, /device:TPU:32 now
where the time goes in v1:
time: 271 us; the launch traced here: 270 us
  waiting for transfers between devices  110 us (41%)
  local copies, waits for them, and re-layouts  53.2 us (20%)
  blocking collectives  49.6 us (18%)
  starting transfers between devices  21.5 us (8%)
  between operations  16.4 us (6%)
  matrix products  12.5 us (5%)
  other arithmetic  6.29 us (2%)
    reduce_scatter x1, waiting for transfers between devices, local(): lax.psum_scatter(partial_term, 'orb', scatter_dimension=1, tiled=True)  55.1 us
    ppermute x8, waiting for transfers between devices, stops_all_end(): shaped.append(lax.ppermute(shaped[-1], axis_name='ao', perm=tray))  51.2 us
    unnamed x64, local copies, waits for them, and re-layouts  45.5 us
    unnamed x1, blocking collectives  23.6 us
    ppermute x7, starting transfers between devices, stops_all_end(): v1.append(lax.ppermute(v1[-1], axis_name='ao', perm=table))  21.4 us
    all_gather x1, blocking collectives, local(): lax.all_gather(occupied_coeff, 'ao', axis=0, tiled=True)  16.6 us
    dot_general x1, matrix products, local(): product = jnp.dot(flat, vir_masked, preferred_element_type=jnp.float32)  9.84 us
    all_to_all x1, blocking collectives, local(): lax.all_to_all(picked, 'orb', split_axis=2, concat_axis=3, tiled=True)  9.44 us
  transfers between devices with their start and end apart: 17, of which 13 were waited for; matrix products, arithmetic and copies ran while one was open for 17% of the time, Pallas kernels for 0%

profile of v1, /device:TPU:32, one launch (start us, length us, event | category | flops | bytes accessed | tf_op | source)
XLA Modules:
  0.0 269.5 jit_solution(3315399587837178091)
XLA Ops:
  8.1 1.4 dynamic-slice
  9.4 0.8 dynamic-update-slice
  10.2 23.6 %all-reduce = bf16[16]{0:T(256)(128)(2,1)S(1)} all-reduce(bf16[16]{0:T(256)(128)(2,1)S(1)} %dynamic-update-slice), channel_id=1, replica_groups=mesh['aux'=8,'ao'=16,'orb'=4] {'ao'}, use_global_device_ids=true, to_apply=%add | all-reduce | flops 16 | bytes 64
  33.9 16.6 %all_gather.11 = bf16[2048,128]{1,0:T(8,128)(2,1)S(1)} all-gather(bf16[128,128]{1,0:T(8,128)(2,1)} %param.10), channel_id=1, replica_groups=mesh['aux'=8,'ao'=16,'orb'=4] {'ao'}, dimensions={0}, use_global_device_ids=true | all-gather | bytes 557056 | tf_op jit(solution)/shard_map/all_gather | solution.py:17
  50.5 0.7 fusion.11
  52.9 9.4 %all_to_all.15 = bf16[1,4,128,128]{3,1,0,2:T(4,128)(2,1)S(1)} all-to-all(bf16[1,4,128,128]{3,1,0,2:T(4,128)(2,1)S(1)} %copy.14), channel_id=1, replica_groups=mesh['aux'=8,'ao'=16,'orb'=4] {'orb'}, dimensions={2} | all-to-all | bytes 262144 | tf_op jit(solution)/shard_map/all_to_all | solution.py:27
  62.5 2.7 %convolution_bitcast_fusion = f32[16,512,1,128]{3,1,0,2:T(8,128)} fusion(bf16[4,32,512,1]{2,1,0,3:T(8,128)(2,1)S(1)} %reshape.69, bf16[16,1,4,32,128]{4,3,2,1,0:T(8,128)(2,1)S(1)} %copy-done), kind=kOutput, calls=%fused_computation.3 | convolution fusion | flops 268435456 | bytes 4849664 | tf_op jit(solution)/shard_map/nkri,pnkrv->pinv/dot_general | solution.py:28
  65.3 55.1 %reduce-scatter.2.cloned.1.call-done = f32[16,128,1,128]{3,1,0,2:T(8,128)} async-done(((f32[16,512,1,128]{3,1,0,2:T(8,128)}), f32[16,128,1,128]{3,1,0,2:T(8,128)}) %reduce-scatter.2.cloned.1.call-update) | async-done | bytes 1048592 | tf_op jit(solution)/shard_map/reduce_scatter | solution.py:31
  120.4 1.4 convert_bitcast_fusion
  121.8 9.8 %collective-permute-done = bf16[16,128,128]{2,1,0:T(8,128)(2,1)S(1)} collective-permute-done((bf16[16,128,128]{2,1,0:T(8,128)(2,1)S(1)}, bf16[16,128,128]{2,1,0:T(8,128)(2,1)S(1)}, u32[]{:S(2)}, u32[]{:S(2)}) %collective-permute-start) | collective-permute-done | bytes 524320 | tf_op jit(solution)/shard_map/ppermute | solution.py:48
  131.6 3.0 %collective-permute-start.8 = (bf16[16,128,128]{2,1,0:T(8,128)(2,1)S(1)}, bf16[16,128,128]{2,1,0:T(8,128)(2,1)S(1)}, u32[]{:S(2)}, u32[]{:S(2)}) collective-permute-start(bf16[16,128,128]{2,1,0:T(8,128)(2,1)S(1)} %convert_bitcast_fusion), channel_id=1, source_target_pairs={{0,60},{4,0},{8,4},{12,8},{16,12},{20,16},{24,20},{28,24},{32,28},... | collective-permute-start | bytes 1572872 | tf_op jit(solution)/shard_map/ppermute | solution.py:50
  134.6 6.9 %collective-permute-done.1 = bf16[16,128,128]{2,1,0:T(8,128)(2,1)S(1)} collective-permute-done((bf16[16,128,128]{2,1,0:T(8,128)(2,1)S(1)}, bf16[16,128,128]{2,1,0:T(8,128)(2,1)S(1)}, u32[]{:S(2)}, u32[]{:S(2)}) %collective-permute-start.1) | collective-permute-done | bytes 524320 | tf_op jit(solution)/shard_map/ppermute | solution.py:48
  141.4 3.0 %collective-permute-start.9 = (bf16[16,128,128]{2,1,0:T(8,128)(2,1)S(1)}, bf16[16,128,128]{2,1,0:T(8,128)(2,1)S(1)}, u32[]{:S(2)}, u32[]{:S(2)}) collective-permute-start(bf16[16,128,128]{2,1,0:T(8,128)(2,1)S(1)} %collective-permute-done.8), channel_id=1, source_target_pairs={{0,60},{4,0},{8,4},{12,8},{16,12},{20,16},{24,20},{28,24},{32,28},... | collective-permute-start | bytes 1572872 | tf_op jit(solution)/shard_map/ppermute | solution.py:50
  144.4 6.9 %collective-permute-done.2 = bf16[16,128,128]{2,1,0:T(8,128)(2,1)S(1)} collective-permute-done((bf16[16,128,128]{2,1,0:T(8,128)(2,1)S(1)}, bf16[16,128,128]{2,1,0:T(8,128)(2,1)S(1)}, u32[]{:S(2)}, u32[]{:S(2)}) %collective-permute-start.2) | collective-permute-done | bytes 524320 | tf_op jit(solution)/shard_map/ppermute | solution.py:48
  151.3 0.8 copy-done.2
  152.1 2.9 %collective-permute-start.10 = (bf16[16,128,128]{2,1,0:T(8,128)(2,1)S(1)}, bf16[16,128,128]{2,1,0:T(8,128)(2,1)S(1)}, u32[]{:S(2)}, u32[]{:S(2)}) collective-permute-start(bf16[16,128,128]{2,1,0:T(8,128)(2,1)S(1)} %collective-permute-done.9), channel_id=1, source_target_pairs={{0,60},{4,0},{8,4},{12,8},{16,12},{20,16},{24,20},{28,24},{32,28},... | collective-permute-start | bytes 1572872 | tf_op jit(solution)/shard_map/ppermute | solution.py:50
  155.0 6.0 %collective-permute-done.3 = bf16[16,128,128]{2,1,0:T(8,128)(2,1)S(1)} collective-permute-done((bf16[16,128,128]{2,1,0:T(8,128)(2,1)S(1)}, bf16[16,128,128]{2,1,0:T(8,128)(2,1)S(1)}, u32[]{:S(2)}, u32[]{:S(2)}) %collective-permute-start.3) | collective-permute-done | bytes 524320 | tf_op jit(solution)/shard_map/ppermute | solution.py:48
  161.7 3.1 %collective-permute-start.11 = (bf16[16,128,128]{2,1,0:T(8,128)(2,1)S(1)}, bf16[16,128,128]{2,1,0:T(8,128)(2,1)S(1)}, u32[]{:S(2)}, u32[]{:S(2)}) collective-permute-start(bf16[16,128,128]{2,1,0:T(8,128)(2,1)S(1)} %collective-permute-done.10), channel_id=1, source_target_pairs={{0,60},{4,0},{8,4},{12,8},{16,12},{20,16},{24,20},{28,24},{32,28},... | collective-permute-start | bytes 1572872 | tf_op jit(solution)/shard_map/ppermute | solution.py:50
  164.9 6.0 %collective-permute-done.4 = bf16[16,128,128]{2,1,0:T(8,128)(2,1)S(1)} collective-permute-done((bf16[16,128,128]{2,1,0:T(8,128)(2,1)S(1)}, bf16[16,128,128]{2,1,0:T(8,128)(2,1)S(1)}, u32[]{:S(2)}, u32[]{:S(2)}) %collective-permute-start.4) | collective-permute-done | bytes 524320 | tf_op jit(solution)/shard_map/ppermute | solution.py:48
  170.9 0.7 collective-permute-done.11
  171.6 0.8 copy-done.8
  172.4 3.1 %collective-permute-start.12 = (bf16[16,128,128]{2,1,0:T(8,128)(2,1)S(1)}, bf16[16,128,128]{2,1,0:T(8,128)(2,1)}, u32[]{:S(2)}, u32[]{:S(2)}) collective-permute-start(bf16[16,128,128]{2,1,0:T(8,128)(2,1)S(1)} %collective-permute-done.11), channel_id=1, source_target_pairs={{0,60},{4,0},{8,4},{12,8},{16,12},{20,16},{24,20},{28,24},{32,28},... | collective-permute-start | bytes 1572872 | tf_op jit(solution)/shard_map/ppermute | solution.py:50
  175.5 5.2 %collective-permute-done.5 = bf16[16,128,128]{2,1,0:T(8,128)(2,1)S(1)} collective-permute-done((bf16[16,128,128]{2,1,0:T(8,128)(2,1)S(1)}, bf16[16,128,128]{2,1,0:T(8,128)(2,1)S(1)}, u32[]{:S(2)}, u32[]{:S(2)}) %collective-permute-start.5) | collective-permute-done | bytes 524320 | tf_op jit(solution)/shard_map/ppermute | solution.py:48
  180.7 1.5 collective-permute-done.12
  182.2 3.2 %collective-permute-start.13 = (bf16[16,128,128]{2,1,0:T(8,128)(2,1)}, bf16[16,128,128]{2,1,0:T(8,128)(2,1)}, u32[]{:S(2)}, u32[]{:S(2)}) collective-permute-start(bf16[16,128,128]{2,1,0:T(8,128)(2,1)} %collective-permute-done.12), channel_id=1, source_target_pairs={{0,60},{4,0},{8,4},{12,8},{16,12},{20,16},{24,20},{28,24},{32,28},... | collective-permute-start | bytes 1572872 | tf_op jit(solution)/shard_map/ppermute | solution.py:50
  185.4 5.2 %collective-permute-done.6 = bf16[16,128,128]{2,1,0:T(8,128)(2,1)} collective-permute-done((bf16[16,128,128]{2,1,0:T(8,128)(2,1)S(1)}, bf16[16,128,128]{2,1,0:T(8,128)(2,1)}, u32[]{:S(2)}, u32[]{:S(2)}) %collective-permute-start.6) | collective-permute-done | bytes 524320 | tf_op jit(solution)/shard_map/ppermute | solution.py:48
  190.7 0.7 convert_element_type.36
  191.5 0.9 collective-permute-done.13
  192.4 3.1 %collective-permute-start.14 = (bf16[16,128,128]{2,1,0:T(8,128)(2,1)}, bf16[16,128,128]{2,1,0:T(8,128)(2,1)S(1)}, u32[]{:S(2)}, u32[]{:S(2)}) collective-permute-start(bf16[16,128,128]{2,1,0:T(8,128)(2,1)} %collective-permute-done.13), channel_id=1, source_target_pairs={{0,60},{4,0},{8,4},{12,8},{16,12},{20,16},{24,20},{28,24},{32,28},... | collective-permute-start | bytes 1572872 | tf_op jit(solution)/shard_map/ppermute | solution.py:50
  195.5 5.2 %collective-permute-done.7 = bf16[16,128,128]{2,1,0:T(8,128)(2,1)} collective-permute-done((bf16[16,128,128]{2,1,0:T(8,128)(2,1)}, bf16[16,128,128]{2,1,0:T(8,128)(2,1)}, u32[]{:S(2)}, u32[]{:S(2)}) %collective-permute-start.7) | collective-permute-done | bytes 524320 | tf_op jit(solution)/shard_map/ppermute | solution.py:48
  200.8 1.9 constant_dynamic-update-slice_fusion.31
  202.7 1.9 constant_dynamic-update-slice_fusion.30
  204.6 1.9 constant_dynamic-update-slice_fusion.29
  206.6 1.9 constant_dynamic-update-slice_fusion.28
  208.5 1.9 constant_dynamic-update-slice_fusion.27
  210.4 1.9 constant_dynamic-update-slice_fusion.26
  212.4 0.9 constant_dynamic-update-slice_fusion.25
  213.2 0.9 constant_dynamic-update-slice_fusion.24
  214.1 2.2 constant_dynamic-update-slice_fusion.23
  216.3 0.9 constant_dynamic-update-slice_fusion.22
  217.2 1.9 constant_dynamic-update-slice_fusion.21
  219.1 1.9 constant_dynamic-update-slice_fusion.20
  221.0 1.9 constant_dynamic-update-slice_fusion.19
  222.9 1.9 constant_dynamic-update-slice_fusion.18
  224.9 1.9 constant_dynamic-update-slice_fusion.17
  226.8 0.9 constant_dynamic-update-slice_fusion.16
  227.7 1.9 constant_dynamic-update-slice_fusion.15
  229.6 1.9 constant_dynamic-update-slice_fusion.14
  231.6 0.9 constant_dynamic-update-slice_fusion.13
  232.5 0.9 constant_dynamic-update-slice_fusion.12
  233.4 0.9 constant_dynamic-update-slice_fusion.11
  234.3 0.9 constant_dynamic-update-slice_fusion.10
  235.2 0.9 constant_dynamic-update-slice_fusion.9
  236.1 0.9 constant_dynamic-update-slice_fusion.8
  237.0 1.0 constant_dynamic-update-slice_fusion.7
  238.0 0.9 constant_dynamic-update-slice_fusion.6
  238.9 0.9 constant_dynamic-update-slice_fusion.5
  239.8 0.9 constant_dynamic-update-slice_fusion.4
  240.7 0.9 constant_dynamic-update-slice_fusion.3
  241.6 2.0 constant_dynamic-update-slice_fusion.2
  243.6 1.9 constant_dynamic-update-slice_fusion.1
  245.5 0.9 constant_dynamic-update-slice_fusion
  246.5 5.8 %broadcast_in_dim.22 = bf16[2048,4,128]{2,1,0:T(4,128)(2,1)S(1)} broadcast(bf16[2048,4]{1,0:T(8,128)(2,1)S(1)} %bitcast.48), dimensions={0,1} | broadcast | bytes 2113536 | tf_op jit(solution)/shard_map/broadcast_in_dim | solution.py:36
  252.3 9.8 %fusion.5 = bf16[16,128,512]{2,1,0:T(8,128)(2,1)} fusion(bf16[2048,512]{1,0:T(8,128)(2,1)} %all-gather.2.cloned.1.call-done, bf16[256,8,4,128]{3,2,1,0:T(4,128)(2,1)S(1)} %bitcast.47, bf16[16,128,4096]{2,1,0:T(8,128)(2,1)} %constant_dynamic-update-slice_fusion, s32[]{:T(128)S(6)} %select_n.18), kind=kOutput, calls=%fused_computation.7 | convolution fusion | flops 4297064448 | bytes 14680068 | tf_op jit(solution)/shard_map/dot_general | solution.py:57
  (60 shorter events, 2.3 us)
Async XLA Ops:
  7.4 55.2 %copy-start = (bf16[16,1,4,32,128]{4,3,2,1,0:T(8,128)(2,1)S(1)}, bf16[16,1,4,32,128]{4,3,2,1,0:T(8,128)(2,1)}, u32[]{:S(2)}) copy-start(bf16[16,1,4,32,128]{4,3,2,1,0:T(8,128)(2,1)} %param.7) | copy-start | bytes 1572868
  7.4 113.0 %reduce-scatter.2.cloned.1.call-start = ((), (), s32[]{:S(2)}) async-start(), calls=%async_computation.2 | async-start | bytes 5242880 | tf_op jit(solution)/shard_map/reduce_scatter | solution.py:31
  65.3 181.1 %all-gather.2.cloned.1.call-start = ((), (), s32[]{:S(2)}) async-start(), calls=%async_computation.3 | async-start | bytes 2359296 | tf_op jit(solution)/shard_map/all_gather | solution.py:35
  120.4 116.6 %copy-start.1 = (f32[16,128,1,128]{3,1,0,2:T(8,128)S(1)}, f32[16,128,1,128]{3,1,0,2:T(8,128)}, u32[]{:S(2)}) copy-start(f32[16,128,1,128]{3,1,0,2:T(8,128)} %reduce-scatter.2.cloned.1.call-done) | copy-start | bytes 3145732
  121.8 9.8 %collective-permute-start = (bf16[16,128,128]{2,1,0:T(8,128)(2,1)S(1)}, bf16[16,128,128]{2,1,0:T(8,128)(2,1)S(1)}, u32[]{:S(2)}, u32[]{:S(2)}) collective-permute-start(bf16[16,128,128]{2,1,0:T(8,128)(2,1)S(1)} %convert_bitcast_fusion), channel_id=1, source_target_pairs={{0,4},{4,8},{8,12},{12,16},{16,20},{20,24},{24,28},{28,32},{32,36}... | collective-permute-start | bytes 1572872 | tf_op jit(solution)/shard_map/ppermute | solution.py:48
  131.6 9.8 %collective-permute-start.1 = (bf16[16,128,128]{2,1,0:T(8,128)(2,1)S(1)}, bf16[16,128,128]{2,1,0:T(8,128)(2,1)S(1)}, u32[]{:S(2)}, u32[]{:S(2)}) collective-permute-start(bf16[16,128,128]{2,1,0:T(8,128)(2,1)S(1)} %collective-permute-done), channel_id=1, source_target_pairs={{0,4},{4,8},{8,12},{12,16},{16,20},{20,24},{24,28},{28,32},{32,36}... | collective-permute-start | bytes 1572872 | tf_op jit(solution)/shard_map/ppermute | solution.py:48
  131.6 9.8 %collective-permute-start.8 = (bf16[16,128,128]{2,1,0:T(8,128)(2,1)S(1)}, bf16[16,128,128]{2,1,0:T(8,128)(2,1)S(1)}, u32[]{:S(2)}, u32[]{:S(2)}) collective-permute-start(bf16[16,128,128]{2,1,0:T(8,128)(2,1)S(1)} %convert_bitcast_fusion), channel_id=1, source_target_pairs={{0,60},{4,0},{8,4},{12,8},{16,12},{20,16},{24,20},{28,24},{32,28},... | collective-permute-start | bytes 1572872 | tf_op jit(solution)/shard_map/ppermute | solution.py:50
  141.4 9.8 %collective-permute-start.2 = (bf16[16,128,128]{2,1,0:T(8,128)(2,1)S(1)}, bf16[16,128,128]{2,1,0:T(8,128)(2,1)S(1)}, u32[]{:S(2)}, u32[]{:S(2)}) collective-permute-start(bf16[16,128,128]{2,1,0:T(8,128)(2,1)S(1)} %collective-permute-done.1), channel_id=1, source_target_pairs={{0,4},{4,8},{8,12},{12,16},{16,20},{20,24},{24,28},{28,32},{32,36}... | collective-permute-start | bytes 1572872 | tf_op jit(solution)/shard_map/ppermute | solution.py:48
  141.4 9.8 %collective-permute-start.9 = (bf16[16,128,128]{2,1,0:T(8,128)(2,1)S(1)}, bf16[16,128,128]{2,1,0:T(8,128)(2,1)S(1)}, u32[]{:S(2)}, u32[]{:S(2)}) collective-permute-start(bf16[16,128,128]{2,1,0:T(8,128)(2,1)S(1)} %collective-permute-done.8), channel_id=1, source_target_pairs={{0,60},{4,0},{8,4},{12,8},{16,12},{20,16},{24,20},{28,24},{32,28},... | collective-permute-start | bytes 1572872 | tf_op jit(solution)/shard_map/ppermute | solution.py:50
  151.2 10.5 %copy-start.4 = (bf16[16,128,128]{2,1,0:T(8,128)(2,1)}, bf16[16,128,128]{2,1,0:T(8,128)(2,1)S(1)}, u32[]{:S(2)}) copy-start(bf16[16,128,128]{2,1,0:T(8,128)(2,1)S(1)} %collective-permute-done.2) | copy-start | bytes 1572868
  151.2 9.8 %collective-permute-start.3 = (bf16[16,128,128]{2,1,0:T(8,128)(2,1)S(1)}, bf16[16,128,128]{2,1,0:T(8,128)(2,1)S(1)}, u32[]{:S(2)}, u32[]{:S(2)}) collective-permute-start(bf16[16,128,128]{2,1,0:T(8,128)(2,1)S(1)} %collective-permute-done.2), channel_id=1, source_target_pairs={{0,4},{4,8},{8,12},{12,16},{16,20},{20,24},{24,28},{28,32},{32,36}... | collective-permute-start | bytes 1572872 | tf_op jit(solution)/shard_map/ppermute | solution.py:48
  151.3 0.8 copy-start.2
  152.1 9.6 %collective-permute-start.10 = (bf16[16,128,128]{2,1,0:T(8,128)(2,1)S(1)}, bf16[16,128,128]{2,1,0:T(8,128)(2,1)S(1)}, u32[]{:S(2)}, u32[]{:S(2)}) collective-permute-start(bf16[16,128,128]{2,1,0:T(8,128)(2,1)S(1)} %collective-permute-done.9), channel_id=1, source_target_pairs={{0,60},{4,0},{8,4},{12,8},{16,12},{20,16},{24,20},{28,24},{32,28},... | collective-permute-start | bytes 1572872 | tf_op jit(solution)/shard_map/ppermute | solution.py:50
  161.1 21.1 %copy-start.10 = (bf16[16,128,128]{2,1,0:T(8,128)(2,1)}, bf16[16,128,128]{2,1,0:T(8,128)(2,1)S(1)}, u32[]{:S(2)}) copy-start(bf16[16,128,128]{2,1,0:T(8,128)(2,1)S(1)} %collective-permute-done.3) | copy-start | bytes 1572868
  161.1 9.8 %collective-permute-start.4 = (bf16[16,128,128]{2,1,0:T(8,128)(2,1)S(1)}, bf16[16,128,128]{2,1,0:T(8,128)(2,1)S(1)}, u32[]{:S(2)}, u32[]{:S(2)}) collective-permute-start(bf16[16,128,128]{2,1,0:T(8,128)(2,1)S(1)} %collective-permute-done.3), channel_id=1, source_target_pairs={{0,4},{4,8},{8,12},{12,16},{16,20},{20,24},{24,28},{28,32},{32,36}... | collective-permute-start | bytes 1572872 | tf_op jit(solution)/shard_map/ppermute | solution.py:48
  161.7 3.1 %copy-start.6 = (bf16[16,128,128]{2,1,0:T(8,128)(2,1)}, bf16[16,128,128]{2,1,0:T(8,128)(2,1)S(1)}, u32[]{:S(2)}) copy-start(bf16[16,128,128]{2,1,0:T(8,128)(2,1)S(1)} %collective-permute-done.10) | copy-start | bytes 1572868
  161.7 9.8 %collective-permute-start.11 = (bf16[16,128,128]{2,1,0:T(8,128)(2,1)S(1)}, bf16[16,128,128]{2,1,0:T(8,128)(2,1)S(1)}, u32[]{:S(2)}, u32[]{:S(2)}) collective-permute-start(bf16[16,128,128]{2,1,0:T(8,128)(2,1)S(1)} %collective-permute-done.10), channel_id=1, source_target_pairs={{0,60},{4,0},{8,4},{12,8},{16,12},{20,16},{24,20},{28,24},{32,28},... | collective-permute-start | bytes 1572872 | tf_op jit(solution)/shard_map/ppermute | solution.py:50
  170.9 14.5 %copy-start.12 = (bf16[16,128,128]{2,1,0:T(8,128)(2,1)}, bf16[16,128,128]{2,1,0:T(8,128)(2,1)S(1)}, u32[]{:S(2)}) copy-start(bf16[16,128,128]{2,1,0:T(8,128)(2,1)S(1)} %collective-permute-done.4) | copy-start | bytes 1572868
  170.9 9.8 %collective-permute-start.5 = (bf16[16,128,128]{2,1,0:T(8,128)(2,1)S(1)}, bf16[16,128,128]{2,1,0:T(8,128)(2,1)S(1)}, u32[]{:S(2)}, u32[]{:S(2)}) collective-permute-start(bf16[16,128,128]{2,1,0:T(8,128)(2,1)S(1)} %collective-permute-done.4), channel_id=1, source_target_pairs={{0,4},{4,8},{8,12},{12,16},{16,20},{20,24},{24,28},{28,32},{32,36}... | collective-permute-start | bytes 1572872 | tf_op jit(solution)/shard_map/ppermute | solution.py:48
  171.5 0.8 copy-start.8
  172.4 9.8 %collective-permute-start.12 = (bf16[16,128,128]{2,1,0:T(8,128)(2,1)S(1)}, bf16[16,128,128]{2,1,0:T(8,128)(2,1)}, u32[]{:S(2)}, u32[]{:S(2)}) collective-permute-start(bf16[16,128,128]{2,1,0:T(8,128)(2,1)S(1)} %collective-permute-done.11), channel_id=1, source_target_pairs={{0,60},{4,0},{8,4},{12,8},{16,12},{20,16},{24,20},{28,24},{32,28},... | collective-permute-start | bytes 1572872 | tf_op jit(solution)/shard_map/ppermute | solution.py:50
  180.7 9.9 %copy-start.14 = (bf16[16,128,128]{2,1,0:T(8,128)(2,1)}, bf16[16,128,128]{2,1,0:T(8,128)(2,1)S(1)}, u32[]{:S(2)}) copy-start(bf16[16,128,128]{2,1,0:T(8,128)(2,1)S(1)} %collective-permute-done.5) | copy-start | bytes 1572868
  180.7 9.9 %collective-permute-start.6 = (bf16[16,128,128]{2,1,0:T(8,128)(2,1)S(1)}, bf16[16,128,128]{2,1,0:T(8,128)(2,1)}, u32[]{:S(2)}, u32[]{:S(2)}) collective-permute-start(bf16[16,128,128]{2,1,0:T(8,128)(2,1)S(1)} %collective-permute-done.5), channel_id=1, source_target_pairs={{0,4},{4,8},{8,12},{12,16},{16,20},{20,24},{24,28},{28,32},{32,36}... | collective-permute-start | bytes 1572872 | tf_op jit(solution)/shard_map/ppermute | solution.py:48
  182.2 10.2 %collective-permute-start.13 = (bf16[16,128,128]{2,1,0:T(8,128)(2,1)}, bf16[16,128,128]{2,1,0:T(8,128)(2,1)}, u32[]{:S(2)}, u32[]{:S(2)}) collective-permute-start(bf16[16,128,128]{2,1,0:T(8,128)(2,1)} %collective-permute-done.12), channel_id=1, source_target_pairs={{0,60},{4,0},{8,4},{12,8},{16,12},{20,16},{24,20},{28,24},{32,28},... | collective-permute-start | bytes 1572872 | tf_op jit(solution)/shard_map/ppermute | solution.py:50
  190.6 10.1 %collective-permute-start.7 = (bf16[16,128,128]{2,1,0:T(8,128)(2,1)}, bf16[16,128,128]{2,1,0:T(8,128)(2,1)}, u32[]{:S(2)}, u32[]{:S(2)}) collective-permute-start(bf16[16,128,128]{2,1,0:T(8,128)(2,1)} %collective-permute-done.6), channel_id=1, source_target_pairs={{0,4},{4,8},{8,12},{12,16},{16,20},{20,24},{24,28},{28,32},{32,36}... | collective-permute-start | bytes 1572872 | tf_op jit(solution)/shard_map/ppermute | solution.py:48
  191.5 40.1 %copy-start.15 = (bf16[16,128,128]{2,1,0:T(8,128)(2,1)S(1)}, bf16[16,128,128]{2,1,0:T(8,128)(2,1)}, u32[]{:S(2)}) copy-start(bf16[16,128,128]{2,1,0:T(8,128)(2,1)} %copy-done.14) | copy-start | bytes 1572868
  191.5 41.0 %copy-start.13 = (bf16[16,128,128]{2,1,0:T(8,128)(2,1)S(1)}, bf16[16,128,128]{2,1,0:T(8,128)(2,1)}, u32[]{:S(2)}) copy-start(bf16[16,128,128]{2,1,0:T(8,128)(2,1)} %copy-done.12) | copy-start | bytes 1572868
  191.5 41.9 %copy-start.11 = (bf16[16,128,128]{2,1,0:T(8,128)(2,1)S(1)}, bf16[16,128,128]{2,1,0:T(8,128)(2,1)}, u32[]{:S(2)}) copy-start(bf16[16,128,128]{2,1,0:T(8,128)(2,1)} %copy-done.10) | copy-start | bytes 1572868
  191.5 42.8 %copy-start.5 = (bf16[16,128,128]{2,1,0:T(8,128)(2,1)S(1)}, bf16[16,128,128]{2,1,0:T(8,128)(2,1)}, u32[]{:S(2)}) copy-start(bf16[16,128,128]{2,1,0:T(8,128)(2,1)} %copy-done.4) | copy-start | bytes 1572868
  191.5 47.5 %copy-start.3 = (bf16[16,128,128]{2,1,0:T(8,128)(2,1)S(1)}, bf16[16,128,128]{2,1,0:T(8,128)(2,1)}, u32[]{:S(2)}) copy-start(bf16[16,128,128]{2,1,0:T(8,128)(2,1)} %copy-done.2) | copy-start | bytes 1572868
  191.5 48.3 %copy-start.7 = (bf16[16,128,128]{2,1,0:T(8,128)(2,1)S(1)}, bf16[16,128,128]{2,1,0:T(8,128)(2,1)}, u32[]{:S(2)}) copy-start(bf16[16,128,128]{2,1,0:T(8,128)(2,1)} %copy-done.6) | copy-start | bytes 1572868
  191.5 49.2 %copy-start.9 = (bf16[16,128,128]{2,1,0:T(8,128)(2,1)S(1)}, bf16[16,128,128]{2,1,0:T(8,128)(2,1)}, u32[]{:S(2)}) copy-start(bf16[16,128,128]{2,1,0:T(8,128)(2,1)} %copy-done.8) | copy-start | bytes 1572868
  192.4 34.4 %collective-permute-start.14 = (bf16[16,128,128]{2,1,0:T(8,128)(2,1)}, bf16[16,128,128]{2,1,0:T(8,128)(2,1)S(1)}, u32[]{:S(2)}, u32[]{:S(2)}) collective-permute-start(bf16[16,128,128]{2,1,0:T(8,128)(2,1)} %collective-permute-done.13), channel_id=1, source_target_pairs={{0,60},{4,0},{8,4},{12,8},{16,12},{20,16},{24,20},{28,24},{32,28},... | collective-permute-start | bytes 1572872 | tf_op jit(solution)/shard_map/ppermute | solution.py:50
Sparse Core Ops, SparseCore 0:
  65.4 54.9 reduce-scatter.1
Sparse Core Ops, SparseCore 1:
  190.7 44.4 all-gather.1
